TPU v7x, 32 devices: a whole 2x2x4 slice. The times are simulated.
32 devices in a mesh: row: 8 (over z, y), col: 4 (over x, core).
Axes of the slice: x: 2, y: 2, z: 4, core: 2. Of those that a mesh axis runs over, the one named last changes fastest.
Arguments:
- start_block: float32 [64, 16, 128], P(('row', 'col')), may hold values from -6 to 6
- blocks: float32 [8, 4, 58, 128, 128], P('row', 'col'), as said below
- slot_row: int32 [8, 4, 58], P('row', 'col'), may hold values from 0 to 7, as said below
- slot_col: int32 [8, 4, 58], P('row', 'col'), may hold values from 0 to 15, as said below
- counts: int32 [8, 4], P('row', 'col'), may hold values from 34 to 58, as said below
Outputs:
- alphas: float32 [2, 16, 16], replicated
- betas: float32 [2, 16, 16], replicated
- next_block: float32 [64, 16, 128], P(('row', 'col'))
Inputs may be any that keep to these rules, and one draw needn't show every extreme that they name: `blocks`: over all cells the live slots list each nonzero block of a symmetric matrix exactly once: block (J, I) is listed exactly when (I, J) is, holding its transpose. Slots at or past a cell's count hold finite values that are no part of H. `counts`: live slots of a cell come first; in every draw some cell has all 58 slots live. `slot_row`: for live slots, the block row within the cell's row group of 8 block rows. `slot_col`: for live slots, the position within the cell's column group of 16 block columns, as in the first step.
All inputs are finite; a program needn't handle non-finite values.
Results may differ from a plain program's by a relative error of at most 0.0003.
Values sent between devices are 32-bit elements; how exact they have to be, the bound alone decides.
A program may use at most 64 MiB of HBM per device.

v0:
```python
import jax
import jax.numpy as jnp
from jax import lax
from jax.sharding import PartitionSpec as P

ITERS = 2
highest = lax.Precision.HIGHEST


def matmul(left, right):
    return jnp.dot(left, right, precision=highest, preferred_element_type=jnp.float32)


def local_gram(left, right):
    return jnp.einsum(
        "bki,bli->kl", left, right, precision=highest, preferred_element_type=jnp.float32
    )


def on_device(start_block, blocks, slot_row, slot_col, counts):
    matrix_tiles = blocks[0, 0]
    rows_local = slot_row[0, 0]
    cols_local = slot_col[0, 0]
    capacity = matrix_tiles.shape[0]
    active = lax.iota(jnp.int32, capacity) < counts[0, 0]
    piece_rows = start_block.shape[0]
    vec_count = start_block.shape[1]
    orbitals = start_block.shape[2]
    row_total = float(piece_rows * lax.axis_size("row") * lax.axis_size("col") * orbitals)
    identity = jnp.eye(vec_count, dtype=jnp.float32)
    start_mean = lax.psum(local_gram(start_block, start_block), ("row", "col")) / row_total
    factor = jnp.linalg.cholesky(start_mean)
    inverse = jax.scipy.linalg.solve_triangular(factor, identity, lower=True)
    vectors = jnp.einsum(
        "kl,bli->bki", inverse, start_block, precision=highest, preferred_element_type=jnp.float32
    )
    previous = jnp.zeros(vectors.shape, jnp.float32)
    beta_prev = jnp.zeros((vec_count, vec_count), jnp.float32)
    alpha_list = []
    beta_list = []
    for iteration in range(ITERS):
        gathered = lax.all_gather(vectors, "row", axis=0, tiled=True)
        operate_product = jnp.einsum(
            "sij,skj->ski",
            matrix_tiles,
            gathered[cols_local],
            precision=highest,
            preferred_element_type=jnp.float32,
        )
        targets = lax.iota(jnp.int32, lax.axis_size("col") * piece_rows)
        selector = ((rows_local[None, :] == targets[:, None]) & active[None, :]).astype(jnp.float32)
        image_block = lax.psum_scatter(
            jnp.einsum(
                "rs,ski->rki",
                selector,
                operate_product,
                precision=highest,
                preferred_element_type=jnp.float32,
            ),
            "col",
            scatter_dimension=0,
            tiled=True,
        )
        stacked = jnp.concatenate([image_block, vectors, previous], axis=1)
        all_means = lax.psum(local_gram(stacked, stacked), ("row", "col")) / row_total
        yy_mean = all_means[:vec_count, :vec_count]
        vy_mean = all_means[vec_count : 2 * vec_count, :vec_count]
        py_mean = all_means[2 * vec_count :, :vec_count]
        vv_mean = all_means[vec_count : 2 * vec_count, vec_count : 2 * vec_count]
        pv_mean = all_means[2 * vec_count :, vec_count : 2 * vec_count]
        pp_mean = all_means[2 * vec_count :, 2 * vec_count :]
        residual = image_block - jnp.einsum(
            "lk,bli->bki", vy_mean, vectors, precision=highest, preferred_element_type=jnp.float32
        )
        residual = residual - jnp.einsum(
            "kl,bli->bki",
            beta_prev,
            previous,
            precision=highest,
            preferred_element_type=jnp.float32,
        )
        gram_mean = yy_mean - matmul(vy_mean.T, vy_mean) - matmul(vy_mean.T, vy_mean)
        gram_mean = gram_mean + matmul(matmul(vy_mean.T, vv_mean), vy_mean)
        gram_mean = gram_mean - matmul(py_mean.T, beta_prev.T) - matmul(beta_prev, py_mean)
        gram_mean = gram_mean + matmul(matmul(vy_mean.T, pv_mean.T), beta_prev.T)
        gram_mean = gram_mean + matmul(matmul(beta_prev, pv_mean), vy_mean)
        gram_mean = gram_mean + matmul(matmul(beta_prev, pp_mean), beta_prev.T)
        factor = jnp.linalg.cholesky(gram_mean)
        beta_block = factor.T
        inverse = jax.scipy.linalg.solve_triangular(factor, identity, lower=True)
        previous = vectors
        vectors = jnp.einsum(
            "kl,bli->bki", inverse, residual, precision=highest, preferred_element_type=jnp.float32
        )
        beta_prev = beta_block
        alpha_list.append(vy_mean)
        beta_list.append(beta_block)
    return (jnp.stack(alpha_list), jnp.stack(beta_list), vectors)


def solution(mesh):
    placed = (
        P(("row", "col"), None, None),
        P("row", "col", None, None, None),
        P("row", "col", None),
        P("row", "col", None),
        P("row", "col"),
    )
    return jax.shard_map(
        on_device,
        mesh=mesh,
        in_specs=placed,
        out_specs=(P(), P(), P(("row", "col"), None, None)),
        check_vma=False,
    )
```

profile of v0, /device:TPU:0, one launch (start us, length us, event | category | flops | bytes accessed | tf_op | source)
XLA Modules:
  0.0 285.7 jit_solution(17474431526224107313)
XLA Ops:
  7.9 0.7 fusion.84
  8.6 0.1 convolution_bitcast_fusion.12
  8.7 42.0 %psum.21 = f32[16,16]{0,1:T(8,128)S(1)} all-reduce(f32[16,16]{0,1:T(8,128)S(1)} %convolution_bitcast_fusion.12), channel_id=1, replica_groups=mesh['row'=8,'col'=4] {'row','col'}, use_global_device_ids=true, to_apply=%region_0.0 | all-reduce | flops 256 | bytes 2048 | tf_op jit(solution)/shard_map/psum | solution.py:31
  50.8 1.5 cholesky.59
  52.3 0.6 compare_reduce_fusion.2
  52.9 0.6 fusion.25
  53.6 1.2 custom-call.7
  54.8 0.2 convolution_bitcast_fusion.11
  55.0 0.1 convolution_bitcast_fusion.8
  55.1 30.6 %all_gather.6 = f32[16,16,128]{2,1,0:T(8,128)S(1)} all-gather(f32[2,16,128]{2,1,0:T(8,128)S(1)} %convolution_bitcast_fusion.8), channel_id=1, replica_groups=mesh['row'=8,'col'=4] {'row'}, dimensions={0}, use_global_device_ids=true | all-gather | bytes 147456 | tf_op jit(solution)/shard_map/all_gather | solution.py:42
  85.7 0.6 gather_fusion
  86.4 8.1 %fusion.2 = f32[58,16,128]{2,1,0:T(8,128)S(1)} fusion(f32[58,16,128]{2,1,0:T(8,128)S(1)} %gather_fusion, f32[1,1,58,128,128]{4,3,2,1,0:T(8,128)} %param.9), kind=kOutput, calls=%fused_computation.4 | convolution fusion | flops 182452224 | bytes 4751360 | tf_op jit(solution)/shard_map/sij,skj->ski/dot_general | solution.py:43
  94.4 0.4 fusion.10
  94.8 0.6 copy.36
  95.6 19.3 %reduce-scatter.3.cloned.1.call-done = f32[2,16,128]{2,1,0:T(8,128)} async-done(((f32[8,16,128]{2,1,0:T(8,128)}), f32[2,16,128]{2,1,0:T(8,128)}) %reduce-scatter.3.cloned.1.call-update) | async-done | bytes 16400 | tf_op jit(solution)/shard_map/reduce_scatter | solution.py:52
  114.9 1.0 convolution_bitcast_fusion.1
  115.9 39.5 %psum.22 = f32[48,48]{0,1:T(8,128)S(1)} all-reduce(f32[48,48]{0,1:T(8,128)S(1)} %convolution_bitcast_fusion.1), channel_id=1, replica_groups=mesh['row'=8,'col'=4] {'row','col'}, use_global_device_ids=true, to_apply=%region_4.0 | all-reduce | flops 2304 | bytes 18432 | tf_op jit(solution)/shard_map/psum | solution.py:65
  155.4 0.2 fusion.50
  155.6 0.2 fusion.30
  155.8 0.2 fusion.52
  156.0 0.2 fusion.32
  156.2 0.2 subtract_subtract_fusion.1
  156.4 0.9 fusion.7
  157.5 0.2 convolution_add_fusion.7
  157.7 0.2 convolution_subtract_fusion.3
  157.9 0.2 convolution_subtract_fusion.2
  158.1 0.1 convolution_add_fusion.6
  158.2 0.2 convolution_add_fusion.5
  158.4 0.1 convolution_add_fusion.4
  158.7 1.5 cholesky.70
  160.2 0.6 compare_reduce_fusion.1
  160.8 0.6 fusion.94
  161.5 1.2 custom-call.8
  162.7 0.2 convolution_bitcast_fusion.10
  162.9 0.1 convolution_bitcast_fusion.5
  163.0 30.7 %all_gather.7 = f32[16,16,128]{2,1,0:T(8,128)S(1)} all-gather(f32[2,16,128]{2,1,0:T(8,128)S(1)} %convolution_bitcast_fusion.5), channel_id=1, replica_groups=mesh['row'=8,'col'=4] {'row'}, dimensions={0}, use_global_device_ids=true | all-gather | bytes 147456 | tf_op jit(solution)/shard_map/all_gather | solution.py:42
  193.8 0.6 gather_fusion.1
  194.4 8.1 %fusion = f32[58,16,128]{2,1,0:T(8,128)S(1)} fusion(f32[58,16,128]{2,1,0:T(8,128)S(1)} %gather_fusion.1, f32[1,1,58,128,128]{4,3,2,1,0:T(8,128)} %param.9), kind=kOutput, calls=%fused_computation.2 | convolution fusion | flops 182452224 | bytes 4751360 | tf_op jit(solution)/shard_map/sij,skj->ski/dot_general | solution.py:43
  202.5 0.4 fusion.8
  202.9 0.6 copy.47
  203.6 20.4 %reduce-scatter.5.cloned.1.call-done = f32[2,16,128]{2,1,0:T(8,128)} async-done(((f32[8,16,128]{2,1,0:T(8,128)}), f32[2,16,128]{2,1,0:T(8,128)}) %reduce-scatter.5.cloned.1.call-update) | async-done | bytes 16400 | tf_op jit(solution)/shard_map/reduce_scatter | solution.py:52
  223.9 1.0 convolution_bitcast_fusion
  224.9 39.5 %psum.23 = f32[48,48]{0,1:T(8,128)S(1)} all-reduce(f32[48,48]{0,1:T(8,128)S(1)} %convolution_bitcast_fusion), channel_id=1, replica_groups=mesh['row'=8,'col'=4] {'row','col'}, use_global_device_ids=true, to_apply=%region_6.9 | all-reduce | flops 2304 | bytes 18432 | tf_op jit(solution)/shard_map/psum | solution.py:65
  264.4 0.8 fusion.44
  265.3 0.9 fusion.26
  266.1 0.2 fusion.46
  266.4 0.2 fusion.28
  266.6 0.2 subtract_subtract_fusion
  266.9 0.9 fusion.5
  267.8 0.8 fusion.4
  268.6 0.2 convolution_add_fusion.3
  268.8 0.9 convolution_subtract_fusion.1
  269.7 0.9 convolution_subtract_fusion
  270.6 0.7 copy.58
  271.2 0.8 convolution_add_fusion.2
  272.1 0.2 convolution_add_fusion.1
  272.3 0.9 convolution_add_fusion
  273.2 1.5 cholesky.81
  274.7 0.6 compare_reduce_fusion
  275.4 0.6 select_bitcast_fusion
  276.0 1.2 custom-call.9
  277.2 0.2 convolution_bitcast_fusion.9
  277.5 0.7 copy.59
  278.2 0.7 convolution_bitcast_fusion.2
  (28 shorter events, 0.8 us)
Async XLA Ops:
  7.2 1.4 copy-start
  7.2 87.3 %copy-start.1 = (s32[1,1,58]{2,1,0:T(1,128)S(1)}, s32[1,1,58]{2,1,0:T(1,128)}, u32[]{:S(2)}) copy-start(s32[1,1,58]{2,1,0:T(1,128)} %param.10) | copy-start | bytes 700
  7.2 107.7 %reduce-scatter.3.cloned.1.call-start = ((), (), s32[]{:S(2)}) async-start(), calls=%async_computation.2 | async-start | bytes 81920 | tf_op jit(solution)/shard_map/reduce_scatter | solution.py:52
  95.5 128.4 %reduce-scatter.5.cloned.1.call-start = ((), (), s32[]{:S(2)}) async-start(), calls=%async_computation.3 | async-start | bytes 81920 | tf_op jit(solution)/shard_map/reduce_scatter | solution.py:52
Sparse Core Ops, SparseCore 0:
  95.6 19.2 reduce-scatter.2
  203.6 20.2 reduce-scatter.4
where the time goes:
time: 287 us; the launch traced here: 286 us
  blocking collectives  182 us (63%)
  waiting for transfers between devices  39.7 us (14%)
  matrix products  31.8 us (11%)
  between operations  14.8 us (5%)
  other arithmetic  12.8 us (4%)
  local copies, waits for them, and re-layouts  4.25 us (1%)
    psum x2, blocking collectives, on_device(): lax.psum(local_gram(stacked, stacked), ('row', 'col')) / row_total  79 us
    all_gather x2, blocking collectives, on_device(): gathered = lax.all_gather(vectors, 'row', axis=0, tiled=True)  61.3 us
    psum x1, blocking collectives, on_device(): lax.psum(local_gram(start_block, start_block), ('row', 'col')) / row_total  42 us
    reduce_scatter x2, waiting for transfers between devices, on_device(): lax.psum_scatter(jnp.einsum('rs,ski->rki', selector, operate_product, pre...  39.7 us
    dot_general x2, matrix products, on_device(): jnp.einsum('sij,skj->ski', matrix_tiles, gathered[cols_local], precision=...  16.1 us
    dot_general x22, matrix products, matmul(): jnp.dot(left, right, precision=highest, preferred_element_type=jnp.float32)  8.28 us
  transfers between devices with their start and end apart: 2, of which 2 were waited for; matrix products, arithmetic and copies ran while one was open for 0% of the time, Pallas kernels for 0%

commit v1 on v0

--- a/solution.py
+++ b/solution.py
@@ -62,7 +62,7 @@
             tiled=True,
         )
         stacked = jnp.concatenate([image_block, vectors, previous], axis=1)
-        all_means = lax.psum(local_gram(stacked, stacked), ("row", "col")) / row_total
+        all_means = lax.psum(lax.psum(local_gram(stacked, stacked), "col"), "row") / row_total
         yy_mean = all_means[:vec_count, :vec_count]
         vy_mean = all_means[vec_count : 2 * vec_count, :vec_count]
         py_mean = all_means[2 * vec_count :, :vec_count]

time: 287 us -> 298 us (1.038)
  blocking collectives: 182 us -> 198 us
  waiting for transfers between devices: 39.7 us -> 35.3 us
    psum x2 -> x4, blocking collectives: 79 us -> 95 us  [the longest x2 74.4 us: on_device(): lax.psum(lax.psum(local_gram(stacked, stacked), 'col'), 'row') / row_total]
    reduce_scatter x2, waiting for transfers between devices: 39.7 us -> 35.3 us  [on_device(): lax.psum_scatter(jnp.einsum('rs,ski->rki', selector, operate_product, pre...]
where the time goes in v1:
time: 298 us; the launch traced here: 297 us
  blocking collectives  198 us (66%)
  waiting for transfers between devices  35.3 us (12%)
  matrix products  31.8 us (11%)
  between operations  14.8 us (5%)
  other arithmetic  12.8 us (4%)
  local copies, waits for them, and re-layouts  4.25 us (1%)
    psum x2, blocking collectives, on_device(): lax.psum(lax.psum(local_gram(stacked, stacked), 'col'), 'row') / row_total  74.4 us
    all_gather x2, blocking collectives, on_device(): gathered = lax.all_gather(vectors, 'row', axis=0, tiled=True)  61.4 us
    psum x1, blocking collectives, on_device(): lax.psum(local_gram(start_block, start_block), ('row', 'col')) / row_total  42 us
    reduce_scatter x2, waiting for transfers between devices, on_device(): lax.psum_scatter(jnp.einsum('rs,ski->rki', selector, operate_product, pre...  35.3 us
    psum x2, blocking collectives, on_device(): lax.psum(local_gram(stacked, stacked), 'col')  20.5 us
    dot_general x2, matrix products, on_device(): jnp.einsum('sij,skj->ski', matrix_tiles, gathered[cols_local], precision=...  16.1 us
    dot_general x22, matrix products, matmul(): jnp.dot(left, right, precision=highest, preferred_element_type=jnp.float32)  8.28 us
  transfers between devices with their start and end apart: 2, of which 2 were waited for; matrix products, arithmetic and copies ran while one was open for 0% of the time, Pallas kernels for 0%

profile of v1, /device:TPU:0, one launch (start us, length us, event | category | flops | bytes accessed | tf_op | source)
XLA Modules:
  0.0 297.4 jit_solution(13366525733376680080)
XLA Ops:
  7.9 0.7 fusion.84
  8.7 42.0 %psum.35 = f32[16,16]{0,1:T(8,128)S(1)} all-reduce(f32[16,16]{0,1:T(8,128)S(1)} %convolution_bitcast_fusion.12), channel_id=1, replica_groups=mesh['row'=8,'col'=4] {'row','col'}, use_global_device_ids=true, to_apply=%region_0.0 | all-reduce | flops 256 | bytes 2048 | tf_op jit(solution)/shard_map/psum | solution.py:31
  50.8 1.5 cholesky.59
  52.3 0.6 compare_reduce_fusion.2
  52.9 0.6 fusion.25
  53.6 1.2 custom-call.7
  54.8 0.2 convolution_bitcast_fusion.11
  55.1 30.6 %all_gather.6 = f32[16,16,128]{2,1,0:T(8,128)S(1)} all-gather(f32[2,16,128]{2,1,0:T(8,128)S(1)} %convolution_bitcast_fusion.8), channel_id=1, replica_groups=mesh['row'=8,'col'=4] {'row'}, dimensions={0}, use_global_device_ids=true | all-gather | bytes 147456 | tf_op jit(solution)/shard_map/all_gather | solution.py:42
  85.7 0.6 gather_fusion
  86.4 8.1 %fusion.2 = f32[58,16,128]{2,1,0:T(8,128)S(1)} fusion(f32[58,16,128]{2,1,0:T(8,128)S(1)} %gather_fusion, f32[1,1,58,128,128]{4,3,2,1,0:T(8,128)} %param.9), kind=kOutput, calls=%fused_computation.4 | convolution fusion | flops 182452224 | bytes 4751360 | tf_op jit(solution)/shard_map/sij,skj->ski/dot_general | solution.py:43
  94.4 0.4 fusion.10
  94.8 0.6 copy.36
  95.6 19.3 %reduce-scatter.3.cloned.1.call-done = f32[2,16,128]{2,1,0:T(8,128)} async-done(((f32[8,16,128]{2,1,0:T(8,128)}), f32[2,16,128]{2,1,0:T(8,128)}) %reduce-scatter.3.cloned.1.call-update) | async-done | bytes 16400 | tf_op jit(solution)/shard_map/reduce_scatter | solution.py:52
  114.9 1.0 convolution_bitcast_fusion.1
  115.9 10.3 %psum.36 = f32[48,48]{0,1:T(8,128)S(1)} all-reduce(f32[48,48]{0,1:T(8,128)S(1)} %convolution_bitcast_fusion.1), channel_id=1, replica_groups=mesh['row'=8,'col'=4] {'col'}, use_global_device_ids=true, to_apply=%region_4.0 | all-reduce | flops 2304 | bytes 18432 | tf_op jit(solution)/shard_map/psum | solution.py:65
  126.1 37.2 %psum.37 = f32[48,48]{0,1:T(8,128)S(1)} all-reduce(f32[48,48]{0,1:T(8,128)S(1)} %psum.36), channel_id=1, replica_groups=mesh['row'=8,'col'=4] {'row'}, use_global_device_ids=true, to_apply=%region_5.0 | all-reduce | flops 2304 | bytes 18432 | tf_op jit(solution)/shard_map/psum | solution.py:65
  163.3 0.2 fusion.50
  163.5 0.2 fusion.30
  163.7 0.2 fusion.52
  163.9 0.2 fusion.32
  164.1 0.2 subtract_subtract_fusion.1
  164.4 0.9 fusion.7
  165.4 0.2 convolution_add_fusion.7
  165.6 0.2 convolution_subtract_fusion.3
  165.8 0.2 convolution_subtract_fusion.2
  166.0 0.1 convolution_add_fusion.6
  166.2 0.2 convolution_add_fusion.5
  166.4 0.1 convolution_add_fusion.4
  166.6 1.5 cholesky.70
  168.1 0.6 compare_reduce_fusion.1
  168.8 0.6 fusion.94
  169.4 1.2 custom-call.8
  170.6 0.2 convolution_bitcast_fusion.10
  170.9 0.1 convolution_bitcast_fusion.5
  171.0 30.8 %all_gather.7 = f32[16,16,128]{2,1,0:T(8,128)S(1)} all-gather(f32[2,16,128]{2,1,0:T(8,128)S(1)} %convolution_bitcast_fusion.5), channel_id=1, replica_groups=mesh['row'=8,'col'=4] {'row'}, dimensions={0}, use_global_device_ids=true | all-gather | bytes 147456 | tf_op jit(solution)/shard_map/all_gather | solution.py:42
  201.8 0.6 gather_fusion.1
  202.4 8.1 %fusion = f32[58,16,128]{2,1,0:T(8,128)S(1)} fusion(f32[58,16,128]{2,1,0:T(8,128)S(1)} %gather_fusion.1, f32[1,1,58,128,128]{4,3,2,1,0:T(8,128)} %param.9), kind=kOutput, calls=%fused_computation.2 | convolution fusion | flops 182452224 | bytes 4751360 | tf_op jit(solution)/shard_map/sij,skj->ski/dot_general | solution.py:43
  210.5 0.4 fusion.8
  210.9 0.6 copy.47
  211.6 16.0 %reduce-scatter.5.cloned.1.call-done = f32[2,16,128]{2,1,0:T(8,128)} async-done(((f32[8,16,128]{2,1,0:T(8,128)}), f32[2,16,128]{2,1,0:T(8,128)}) %reduce-scatter.5.cloned.1.call-update) | async-done | bytes 16400 | tf_op jit(solution)/shard_map/reduce_scatter | solution.py:52
  227.6 1.0 convolution_bitcast_fusion
  228.6 10.3 %psum.38 = f32[48,48]{0,1:T(8,128)S(1)} all-reduce(f32[48,48]{0,1:T(8,128)S(1)} %convolution_bitcast_fusion), channel_id=1, replica_groups=mesh['row'=8,'col'=4] {'col'}, use_global_device_ids=true, to_apply=%region_7.10 | all-reduce | flops 2304 | bytes 18432 | tf_op jit(solution)/shard_map/psum | solution.py:65
  238.9 37.2 %psum.39 = f32[48,48]{0,1:T(8,128)S(1)} all-reduce(f32[48,48]{0,1:T(8,128)S(1)} %psum.38), channel_id=1, replica_groups=mesh['row'=8,'col'=4] {'row'}, use_global_device_ids=true, to_apply=%region_8.11 | all-reduce | flops 2304 | bytes 18432 | tf_op jit(solution)/shard_map/psum | solution.py:65
  276.1 0.8 fusion.44
  276.9 0.9 fusion.26
  277.8 0.2 fusion.46
  278.0 0.2 fusion.28
  278.2 0.2 subtract_subtract_fusion
  278.5 0.9 fusion.5
  279.4 0.8 fusion.4
  280.3 0.2 convolution_add_fusion.3
  280.5 0.9 convolution_subtract_fusion.1
  281.3 0.9 convolution_subtract_fusion
  282.2 0.7 copy.58
  282.9 0.8 convolution_add_fusion.2
  283.7 0.2 convolution_add_fusion.1
  283.9 0.9 convolution_add_fusion
  284.9 1.5 cholesky.81
  286.4 0.6 compare_reduce_fusion
  287.0 0.6 select_bitcast_fusion
  287.7 1.2 custom-call.9
  288.9 0.2 convolution_bitcast_fusion.9
  289.1 0.7 copy.59
  289.8 0.7 convolution_bitcast_fusion.2
  (30 shorter events, 1.1 us)
Async XLA Ops:
  7.2 1.4 copy-start
  7.2 87.3 %copy-start.1 = (s32[1,1,58]{2,1,0:T(1,128)S(1)}, s32[1,1,58]{2,1,0:T(1,128)}, u32[]{:S(2)}) copy-start(s32[1,1,58]{2,1,0:T(1,128)} %param.10) | copy-start | bytes 700
  7.2 107.7 %reduce-scatter.3.cloned.1.call-start = ((), (), s32[]{:S(2)}) async-start(), calls=%async_computation.2 | async-start | bytes 81920 | tf_op jit(solution)/shard_map/reduce_scatter | solution.py:52
  95.5 132.1 %reduce-scatter.5.cloned.1.call-start = ((), (), s32[]{:S(2)}) async-start(), calls=%async_computation.3 | async-start | bytes 81920 | tf_op jit(solution)/shard_map/reduce_scatter | solution.py:52
Sparse Core Ops, SparseCore 0:
  95.6 19.2 reduce-scatter.2
  211.7 15.8 reduce-scatter.4
